TPU v7x, 32 devices: a whole 2x2x4 slice. The times are simulated.
32 devices in a mesh: replica: 8 (over y, x, core), shard: 4 (over z).
Axes of the slice: x: 2, y: 2, z: 4, core: 2. Of those that a mesh axis runs over, the one named last changes fastest.
Arguments:
- inputs: float32 [64, 512, 1024], P(('replica', 'shard')), may hold values from -6 to 6
- lengths: int32 [64], P(('replica', 'shard')), may hold values from 1 to 512, 24576 in all
- cotangent: float32 [64, 512, 1024], P(('replica', 'shard')), may hold values from -6 to 6
- w_in: bfloat16 [2, 1024, 4384], P(None, 'shard'), may hold values from -0.1875 to 0.1875
- w_out: bfloat16 [2, 2048, 1024], P(None, 'shard'), may hold values from -0.125 to 0.125
- norm_gain: float32 [2, 1024], replicated, may hold values from 0.5 to 1.5
- conv_weight: float32 [2, 4, 2304], replicated, may hold values from -3 to 3
- conv_bias: float32 [2, 2304], replicated, may hold values from -3 to 3
- gate_gain: float32 [2, 2048], replicated, may hold values from 0.5 to 1.5
- dt_bias: float32 [2, 32], replicated, may hold values from -6.9 to -2.3
- a_log: float32 [2, 32], replicated, may hold values from 0 to 2.77
- skip: float32 [2, 32], replicated, may hold values from 0.5 to 1.5
Outputs:
- output: float32 [64, 512, 1024], P(('replica', 'shard'))
- input_grad: float32 [64, 512, 1024], P(('replica', 'shard'))
- grad_w_in: float32 [2, 1024, 4384], P(None, 'shard')
- grad_w_out: float32 [2, 2048, 1024], P(None, 'shard')
- grad_norm_gain: float32 [2, 1024], replicated
- grad_conv_weight: float32 [2, 4, 2304], replicated
- grad_conv_bias: float32 [2, 2304], replicated
- grad_gate_gain: float32 [2, 2048], replicated
- grad_dt_bias: float32 [2, 32], replicated
- grad_a_log: float32 [2, 32], replicated
- grad_skip: float32 [2, 32], replicated
Inputs may be any that keep to these rules, and one draw needn't show every extreme that they name: `lengths`: every sequence has at least one token; the longest in each draw has exactly 512.
All inputs are finite; a program needn't handle non-finite values. No bound on the sum of `lengths` on one device may be relied on, other than what follows from the above.
Results may differ from a plain program's by a relative error of at most 0.028.
Values may be sent and summed in bfloat16 or wider, within the bound.
No kernel may reach another device: no remote copies, remote signals or barrier semaphores. Data moves between devices by JAX's collectives and lax.ppermute only.
A program may use at most 320 MiB of HBM per device.

v0:
```python
import jax
import jax.numpy as jnp
from jax import lax
from jax.sharding import PartitionSpec as P

DI = 2048
HEADS = 32
HEAD_DIM = 64
STATE = 128
CONV = 4
SPAN = 256
LEN = 512
EPSILON = 1e-05
HIGHEST = lax.Precision.HIGHEST


def rms_scale(values, gain):
    return values * lax.rsqrt(jnp.mean(values * values, axis=-1, keepdims=True) + EPSILON) * gain


def span_scan(inner_x, step_size, rate, b_input, c_output):
    seq_len = inner_x.shape[0]
    blocks = seq_len // SPAN
    logs = (step_size * rate[None, :]).reshape(blocks, SPAN, HEADS)
    cum_logs = jnp.cumsum(logs, axis=1)
    scaled_x = (inner_x * step_size[:, :, None]).reshape(blocks, SPAN, HEADS, HEAD_DIM)
    b_blocks = b_input.reshape(blocks, SPAN, STATE)
    c_blocks = c_output.reshape(blocks, SPAN, STATE)
    scores = jnp.einsum("cqn,ckn->cqk", c_blocks, b_blocks, precision=HIGHEST)
    row_index = lax.broadcasted_iota(jnp.int32, (SPAN, SPAN), 0)
    col_index = lax.broadcasted_iota(jnp.int32, (SPAN, SPAN), 1)
    causal = (row_index >= col_index)[None, None, :, :]
    cum_heads = jnp.transpose(cum_logs, (0, 2, 1))
    log_gaps = cum_heads[:, :, :, None] - cum_heads[:, :, None, :]
    decays = jnp.where(causal, jnp.exp(jnp.where(causal, log_gaps, 0.0)), 0.0)
    mixing = decays * scores[:, None, :, :]
    intra = jnp.einsum("chqk,ckhp->cqhp", mixing, scaled_x, precision=HIGHEST)
    to_end = jnp.exp(cum_logs[:, -1:, :] - cum_logs)
    states = jnp.einsum(
        "ckhp,ckn->chpn", scaled_x * to_end[:, :, :, None], b_blocks, precision=HIGHEST
    )
    totals = jnp.exp(cum_logs[:, -1, :])
    carried = jnp.zeros((HEADS, HEAD_DIM, STATE), jnp.float32)
    previous = []
    for block in range(blocks):
        previous.append(carried)
        carried = totals[block][:, None, None] * carried + states[block]
    previous = jnp.stack(previous)
    inter = (
        jnp.einsum("cqn,chpn->cqhp", c_blocks, previous, precision=HIGHEST)
        * jnp.exp(cum_logs)[:, :, :, None]
    )
    return (intra + inter).reshape(seq_len, HEADS, HEAD_DIM)


def mix_one(projected, conv_weight, conv_bias, gate_gain, dt_bias, a_log, skip):
    seq_len = projected.shape[0]
    gate_part = projected[:, :DI]
    conv_in = projected[:, DI : 2 * DI + 2 * STATE]
    raw_step = projected[:, 2 * DI + 2 * STATE :]
    padded = jnp.pad(conv_in, ((CONV - 1, 0), (0, 0)))
    pre_act = conv_bias[None, :] + conv_weight[0][None, :] * padded[0:seq_len]
    for offset in range(1, CONV):
        pre_act = pre_act + conv_weight[offset][None, :] * padded[offset : offset + seq_len]
    act = jax.nn.silu(pre_act)
    inner_x = act[:, :DI].reshape(seq_len, HEADS, HEAD_DIM)
    b_input = act[:, DI : DI + STATE]
    c_output = act[:, DI + STATE :]
    step_size = jax.nn.softplus(raw_step + dt_bias[None, :])
    scanned = span_scan(inner_x, step_size, -jnp.exp(a_log), b_input, c_output)
    scanned = scanned + skip[None, :, None] * inner_x
    gated = scanned.reshape(seq_len, DI) * jax.nn.silu(gate_part)
    return rms_scale(gated, gate_gain)


def mix_part(projected, extras):
    by_seq = projected.reshape(-1, LEN, projected.shape[1])
    one_seq = jax.checkpoint(lambda row: mix_one(row, *extras))
    return lax.map(one_seq, by_seq).reshape(projected.shape[0], DI)


def contract_rows(left, right):
    return lax.dot_general(
        left, right, (((0,), (0,)), ((), ())), preferred_element_type=jnp.float32
    )


def contract_cols(left, right):
    return lax.dot_general(
        left, right, (((1,), (1,)), ((), ())), preferred_element_type=jnp.float32
    )


def per_device(
    inputs,
    lengths,
    cotangent,
    w_in,
    w_out,
    norm_gain,
    conv_weight,
    conv_bias,
    gate_gain,
    dt_bias,
    a_log,
    skip,
):
    slot_count, seq_len, width = inputs.shape
    row_total = slot_count * seq_len
    places = lax.broadcasted_iota(jnp.int32, (slot_count, seq_len), 1)
    valid_mask = (places < lengths[:, None]).astype(jnp.float32).reshape(row_total, 1)
    layer_count = w_in.shape[0]
    hidden = inputs.reshape(row_total, width)
    saved = []
    for layer in range(layer_count):
        full_in, full_out = (
            lax.all_gather(w_in[layer], "shard", axis=0, tiled=True),
            lax.all_gather(w_out[layer], "shard", axis=0, tiled=True),
        )
        extras = (
            conv_weight[layer],
            conv_bias[layer],
            gate_gain[layer],
            dt_bias[layer],
            a_log[layer],
            skip[layer],
        )
        normed_full, norm_pull = jax.vjp(rms_scale, hidden, norm_gain[layer])
        normed = normed_full.astype(jnp.bfloat16)
        projected = jnp.dot(normed, full_in, preferred_element_type=jnp.float32)
        mixed_full, mix_pull = jax.vjp(mix_part, projected, extras)
        mixed = mixed_full.astype(jnp.bfloat16)
        branch = jnp.dot(mixed, full_out, preferred_element_type=jnp.float32)
        hidden = hidden + valid_mask * branch
        saved.append((normed, mixed, norm_pull, mix_pull, None, None))
    grad_stream = cotangent.reshape(row_total, width)
    in_parts = [None] * layer_count
    out_parts = [None] * layer_count
    gain_parts = [None] * layer_count
    extra_parts = [None] * layer_count
    for layer in reversed(range(layer_count)):
        normed, mixed, norm_pull, mix_pull, full_in, full_out = saved[layer]
        full_in, full_out = (
            lax.all_gather(w_in[layer], "shard", axis=0, tiled=True),
            lax.all_gather(w_out[layer], "shard", axis=0, tiled=True),
        )
        d_branch = (valid_mask * grad_stream).astype(jnp.bfloat16)
        local_out = contract_rows(mixed, d_branch)
        d_mixed = contract_cols(d_branch, full_out)
        d_projected, d_extras = mix_pull(d_mixed)
        d_proj_low = d_projected.astype(jnp.bfloat16)
        local_in = contract_rows(normed, d_proj_low)
        d_normed = contract_cols(d_proj_low, full_in)
        d_hidden, d_gain = norm_pull(d_normed)
        grad_stream = grad_stream + d_hidden
        owned_in, owned_out = (
            lax.psum_scatter(
                local_in.astype(jnp.bfloat16), "shard", scatter_dimension=0, tiled=True
            ).astype(jnp.float32),
            lax.psum_scatter(
                local_out.astype(jnp.bfloat16), "shard", scatter_dimension=0, tiled=True
            ).astype(jnp.float32),
        )
        owned_in, owned_out = (
            lax.psum(owned_in.astype(jnp.bfloat16), "replica").astype(jnp.float32),
            lax.psum(owned_out.astype(jnp.bfloat16), "replica").astype(jnp.float32),
        )
        in_parts[layer] = owned_in
        out_parts[layer] = owned_out
        gain_parts[layer] = d_gain
        extra_parts[layer] = d_extras
    small_local = (
        jnp.stack(gain_parts),
        jnp.stack([item[0] for item in extra_parts]),
        jnp.stack([item[1] for item in extra_parts]),
        jnp.stack([item[2] for item in extra_parts]),
        jnp.stack([item[3] for item in extra_parts]),
        jnp.stack([item[4] for item in extra_parts]),
        jnp.stack([item[5] for item in extra_parts]),
    )
    summed = lax.psum(
        (
            small_local[0],
            small_local[1],
            small_local[2],
            small_local[3],
            small_local[4],
            small_local[5],
            small_local[6],
        ),
        ("replica", "shard"),
    )
    return (
        hidden.reshape(slot_count, seq_len, width),
        grad_stream.reshape(slot_count, seq_len, width),
        jnp.stack(in_parts),
        jnp.stack(out_parts),
        summed[0],
        summed[1],
        summed[2],
        summed[3],
        summed[4],
        summed[5],
        summed[6],
    )


def solution(mesh):
    in_specs = (
        P(("replica", "shard"), None, None),
        P(("replica", "shard")),
        P(("replica", "shard"), None, None),
        P(None, "shard", None),
        P(None, "shard", None),
        P(),
        P(),
        P(),
        P(),
        P(),
        P(),
        P(),
    )
    out_specs = (
        P(("replica", "shard"), None, None),
        P(("replica", "shard"), None, None),
        P(None, "shard", None),
        P(None, "shard", None),
        P(),
        P(),
        P(),
        P(),
        P(),
        P(),
        P(),
    )
    return jax.shard_map(
        per_device, mesh=mesh, in_specs=in_specs, out_specs=out_specs, check_vma=False
    )
```

profile of v0, /device:TPU:8, one launch (start us, length us, event | category | flops | bytes accessed | tf_op | source)
XLA Modules:
  0.0 2129.3 jit_solution(17221925567403622853)
XLA Ops:
  25.7 64.1 %all-gather.15.cloned.1.call-done = bf16[1,2048,1024]{2,1,0:T(8,128)(2,1)} async-done(((bf16[1,512,1024]{2,1,0:T(8,128)(2,1)}), bf16[1,2048,1024]{2,1,0:T(8,128)(2,1)}) %all-gather.15.cloned.1.call-update) | async-done | bytes 4194320 | tf_op jit(solution)/shard_map/all_gather | solution.py:118
  89.8 11.7 fusion.234
  101.5 147.4 %all-gather.9.cloned.1.call-done = bf16[1,1024,4384]{1,2,0:T(8,128)(2,1)} async-done(((bf16[1,256,4384]{1,2,0:T(8,128)(2,1)}), bf16[1,1024,4384]{1,2,0:T(8,128)(2,1)}) %all-gather.9.cloned.1.call-update) | async-done | bytes 8978448 | tf_op jit(solution)/shard_map/all_gather | solution.py:117
  248.9 17.7 fusion.228
  269.1 195.3 %while.84 = (s32[]{:T(128)}, bf16[2,512,2048]{2,1,0:T(8,128)(2,1)}, f32[1,2304]{1,0:T(1,128)S(1)}, f32[1,2304]{1,0:T(1,128)S(1)}, f32[2,512,4384]{1,2,0:T(8,128)...) while((s32[]{:T(128)}, bf16[2,512,2048]{2,1,0:T(8,128)(2,1)}, ...), condition=%wide.region_5.6_spmd.clone.clone, body=%wide.region_1.5_spmd.clone.clone.sunk | while | flops 5888705024 | bytes 198113264 | solution.py:79
  284.8 12.7 divide_multiply_fusion.4
  308.1 11.1 broadcast_multiply_fusion.29
  325.1 20.4 fusion.414
  382.2 12.7 divide_multiply_fusion.4
  405.5 11.1 broadcast_multiply_fusion.29
  422.6 20.4 fusion.414
  464.5 11.2 multiply_reduce_fusion.34
  475.8 12.4 all-gather.13.cloned.1.call-done
  488.2 13.7 fusion.226
  512.7 439.3 %while.86 = (s32[]{:T(128)}, f32[2304]{0:T(1024)}, f32[4,2304]{1,0:T(4,128)}, f32[32]{0:T(128)}, f32[32]{0:T(128)}, /*index=5*/f32[32]{0:T(128)}, f32[2048]{0:T(...) while((s32[]{:T(128)}, f32[2304]{0:T(1024)}, ...), condition=%wide.region_37.39_spmd.clone, body=%wide.region_12.38_spmd.clone.sunk | while | flops 18517338112 | bytes 734076864 | solution.py:79
  523.1 8.2 fusion.448
  557.1 19.7 bitcast_add_fusion.17
  604.7 8.9 fusion.457
  613.6 26.5 %fusion.456 = (f32[2,32,256]{2,1,0:T(8,128)S(1)}, f32[2,32,256]{2,1,0:T(8,128)}, f32[2,256,256]{2,1,0:T(8,128)S(1)}) fusion(f32[2,256,256]{2,1,0:T(8,128)S(1)} %fusion.452, f32[2,32,256]{2,1,0:T(8,128)S(1)} %get-tuple-element.2367, pred[256,256]{1,0:T(8,128)(4,1)S(1)} %iota_compare_fusion.5, f32[2,256,32,64]{1,0,3,2:T(2,128)} %reshape.1287, ...), kind=kOutput, calls=%fused_computation.112.clone.1 | convolution fusion | flops 3268247552 | bytes 9764864 | tf_op jit(solution)/shard_map/transpose(jvp())/while/body/eval_jaxpr/checkpoint/chqk,ckhp->cqhp/dot_general | solution.py:37
  660.0 15.0 bitcast_add_fusion.18
  690.2 10.1 broadcast_multiply_fusion.34
  700.3 7.9 pad_add_fusion.8
  739.9 8.2 fusion.448
  773.9 19.7 bitcast_add_fusion.17
  821.5 8.9 fusion.457
  830.4 26.5 %fusion.456 = (f32[2,32,256]{2,1,0:T(8,128)S(1)}, f32[2,32,256]{2,1,0:T(8,128)}, f32[2,256,256]{2,1,0:T(8,128)S(1)}) fusion(f32[2,256,256]{2,1,0:T(8,128)S(1)} %fusion.452, f32[2,32,256]{2,1,0:T(8,128)S(1)} %get-tuple-element.2367, pred[256,256]{1,0:T(8,128)(4,1)S(1)} %iota_compare_fusion.5, f32[2,256,32,64]{1,0,3,2:T(2,128)} %reshape.1287, ...), kind=kOutput, calls=%fused_computation.112.clone.1 | convolution fusion | flops 3268247552 | bytes 9764864 | tf_op jit(solution)/shard_map/transpose(jvp())/while/body/eval_jaxpr/checkpoint/chqk,ckhp->cqhp/dot_general | solution.py:37
  876.8 15.0 bitcast_add_fusion.18
  907.0 10.1 broadcast_multiply_fusion.34
  917.1 7.9 pad_add_fusion.8
  952.1 11.8 copy.326
  963.9 16.9 multiply_reduce_fusion.32
  993.6 211.0 %while.85 = (s32[]{:T(128)}, bf16[2,512,2048]{2,1,0:T(8,128)(2,1)}, f32[1,2304]{1,0:T(1,128)S(1)}, f32[1,2304]{1,0:T(1,128)S(1)}, f32[2,512,4384]{1,2,0:T(8,128)...) while((s32[]{:T(128)}, bf16[2,512,2048]{2,1,0:T(8,128)(2,1)}, ...), condition=%wide.region_11.12_spmd.clone.clone, body=%wide.region_7.11_spmd.clone.clone.sunk | while | flops 5888705024 | bytes 198113264 | solution.py:79
  1025.2 12.7 divide_multiply_fusion.5
  1048.4 11.1 broadcast_multiply_fusion.31
  1065.4 20.4 fusion.427
  1122.4 12.7 divide_multiply_fusion.5
  1145.6 11.0 broadcast_multiply_fusion.31
  1162.5 20.4 fusion.427
  1204.6 10.1 bitcast_convert_fusion.1
  1215.4 16.5 convolution_convert_fusion
  1232.6 11.4 fusion.238
  1248.2 460.2 %while.87 = (s32[]{:T(128)}, f32[2304]{0:T(1024)}, f32[4,2304]{1,0:T(4,128)}, f32[32]{0:T(128)}, f32[32]{0:T(128)}, /*index=5*/f32[32]{0:T(128)}, f32[2048]{0:T(...) while((s32[]{:T(128)}, f32[2304]{0:T(1024)}, ...), condition=%wide.region_64.66_spmd.clone, body=%wide.region_39.65_spmd.clone.sunk | while | flops 18517338112 | bytes 706551744 | solution.py:79
  1248.4 8.3 dynamic-slice_bitcast_fusion.14
  1268.4 8.2 fusion.480
  1302.3 19.7 bitcast_add_fusion.19
  1350.2 8.9 fusion.489
  1359.2 26.5 %fusion.488 = (f32[2,32,256]{2,1,0:T(8,128)S(1)}, f32[2,32,256]{2,1,0:T(8,128)}, f32[2,256,256]{2,1,0:T(8,128)S(1)}) fusion(f32[2,256,256]{2,1,0:T(8,128)S(1)} %fusion.484, f32[2,32,256]{2,1,0:T(8,128)S(1)} %get-tuple-element.2434, pred[256,256]{1,0:T(8,128)(4,1)S(1)} %iota_compare_fusion.6, f32[2,256,32,64]{1,0,3,2:T(2,128)} %reshape.1293, ...), kind=kOutput, calls=%fused_computation.257.clone.1 | convolution fusion | flops 3268247552 | bytes 9764864 | tf_op jit(solution)/shard_map/transpose(jvp())/while/body/eval_jaxpr/checkpoint/chqk,ckhp->cqhp/dot_general | solution.py:37
  1405.7 15.0 bitcast_add_fusion.20
  1435.9 10.0 broadcast_multiply_fusion.37
  1475.2 8.3 dynamic-slice_bitcast_fusion.14
  1495.0 8.2 fusion.480
  1528.9 19.7 bitcast_add_fusion.19
  1576.7 8.9 fusion.489
  1585.6 26.5 %fusion.488 = (f32[2,32,256]{2,1,0:T(8,128)S(1)}, f32[2,32,256]{2,1,0:T(8,128)}, f32[2,256,256]{2,1,0:T(8,128)S(1)}) fusion(f32[2,256,256]{2,1,0:T(8,128)S(1)} %fusion.484, f32[2,32,256]{2,1,0:T(8,128)S(1)} %get-tuple-element.2434, pred[256,256]{1,0:T(8,128)(4,1)S(1)} %iota_compare_fusion.6, f32[2,256,32,64]{1,0,3,2:T(2,128)} %reshape.1293, ...), kind=kOutput, calls=%fused_computation.257.clone.1 | convolution fusion | flops 3268247552 | bytes 9764864 | tf_op jit(solution)/shard_map/transpose(jvp())/while/body/eval_jaxpr/checkpoint/chqk,ckhp->cqhp/dot_general | solution.py:37
  1632.0 15.0 bitcast_add_fusion.20
  1662.2 10.0 broadcast_multiply_fusion.37
  1708.4 15.8 bitcast_convert_fusion
  1724.3 155.1 %reduce-scatter.5.cloned.1.call-done = bf16[256,4384]{0,1:T(8,128)(2,1)} async-done(((bf16[1024,4384]{0,1:T(8,128)(2,1)}), bf16[256,4384]{0,1:T(8,128)(2,1)}) %reduce-scatter.5.cloned.1.call-update) | async-done | bytes 2244624 | tf_op jit(solution)/shard_map/reduce_scatter | solution.py:157
  1879.6 11.9 copy.328
  1891.6 17.5 fusion.244
  1917.5 42.3 %all-reduce.44 = (f32[2,1024]{1,0:T(2,128)}, f32[2,2304]{1,0:T(2,128)}, f32[2,2048]{1,0:T(2,128)}, f32[2,32]{1,0:T(2,128)}, f32[2,32]{1,0:T(2,128)}, /*index=5*/f32[2,32]{1,0:T(2,128)}) all-reduce(f32[2,1024]{1,0:T(2,128)S(1)} %pad_maximum_fusion.3, ...), channel_id=1, replica_groups=mesh['replica'=8,'shard'=4] {'replica','shard'}, use_global_device_ids=true, to_apply=%region_76.78 | all-reduce | flops 10944 | bytes 87552 | tf_op jit(solution)/shard_map/psum | solution.py:181
  1959.8 12.0 multiply_add_fusion.6
  1971.8 21.3 %all-reduce.51.cloned.1.call-done = (bf16[1,256,4384]{1,2,0:T(8,128)(2,1)}, bf16[1,256,4384]{1,2,0:T(8,128)(2,1)}, bf16[1,512,1024]{2,1,0:T(8,128)(2,1)}, bf16[1,512,1024]{2,1,0:T(8,128)(2,1)}) async-done(((bf16[1,256,4384]{1,2,0:T(8,128)(2,1)}, bf16[1,256,4384]{1,2,0:T(8,128)(2,1)}, bf16[1,512,1024]{2,1,0:T(8,128)(2,1)}, bf16[1,512,1024]{2,1,0:T(8,128)(2,1)}), (bf16[1,256,4384]{1,2,0:T(8,128)(2,1)}, ...) | async-done | bytes 6586384 | tf_op jit(solution)/shard_map/psum | solution.py:165
  2002.1 118.3 %all-reduce.49.cloned.1.call-done = f32[2,4,2304]{2,1,0:T(4,128)} async-done(((f32[2,4,2304]{2,1,0:T(4,128)}), f32[2,4,2304]{2,1,0:T(4,128)}) %all-reduce.49.cloned.1.call-update) | async-done | bytes 73744 | tf_op jit(solution)/shard_map/psum | solution.py:181
  (1073 shorter events, 776.8 us)
Async XLA Ops:
  7.2 82.6 %all-gather.15.cloned.1.call-start = ((), (), s32[]{:S(2)}) async-start(), calls=%async_computation.12 | async-start | bytes 5242880 | tf_op jit(solution)/shard_map/all_gather | solution.py:118
  10.3 238.6 %all-gather.9.cloned.1.call-start = ((), (), s32[]{:S(2)}) async-start(), calls=%async_computation.9 | async-start | bytes 11223040 | tf_op jit(solution)/shard_map/all_gather | solution.py:117
  15.2 9.9 copy-start.140
  15.2 9.9 copy-start.141
  15.2 449.3 %all-gather.11.cloned.1.call-start = ((), (), s32[]{:S(2)}) async-start(), calls=%async_computation.10 | async-start | bytes 5242880 | tf_op jit(solution)/shard_map/all_gather | solution.py:118
  15.9 472.3 %all-gather.13.cloned.1.call-start = ((), (), s32[]{:S(2)}) async-start(), calls=%async_computation.11 | async-start | bytes 11223040 | tf_op jit(solution)/shard_map/all_gather | solution.py:117
  16.5 1707.7 %reduce-scatter.9.cloned.1.call-start = ((), (), s32[]{:S(2)}) async-start(), calls=%async_computation.6 | async-start | bytes 5242880 | tf_op jit(solution)/shard_map/reduce_scatter | solution.py:160
  18.5 230.4 %copy-start.121 = (f32[1,1024]{1,0:T(1,128)}, f32[1,1024]{1,0:T(1,128)S(1)}, u32[]{:S(2)}) copy-start(f32[1,1024]{1,0:T(1,128)S(1)} %get-tuple-element.1838) | copy-start | bytes 12292
  22.1 226.9 %copy-start.131 = (f32[2,512]{1,0:T(2,128)}, f32[2,512]{1,0:T(2,128)S(1)}, u32[]{:S(2)}) copy-start(f32[2,512]{1,0:T(2,128)S(1)} %get-tuple-element.1840) | copy-start | bytes 12292
  24.5 76.9 %copy-start.136 = (f32[2,512]{1,0:T(2,128)}, f32[2,512]{1,0:T(2,128)S(1)}, u32[]{:S(2)}) copy-start(f32[2,512]{1,0:T(2,128)S(1)} %get-tuple-element.1853) | copy-start | bytes 12292
  269.1 195.4 %copy-start.132 = (f32[1,4,2,128]{3,1,2,0:T(4,128)S(1)}, f32[1,4,2,128]{3,1,2,0:T(4,128)}, u32[]{:S(2)}) copy-start(f32[1,4,2,128]{3,1,2,0:T(4,128)} %copy.386) | copy-start | bytes 12292
  464.5 11.3 copy-start.35
  464.5 11.3 copy-start.76
  464.5 23.7 %copy-start.123 = (f32[1,1024]{1,0:T(1,128)S(1)}, f32[1,1024]{1,0:T(1,128)}, u32[]{:S(2)}) copy-start(f32[1,1024]{1,0:T(1,128)} %get-tuple-element.1837) | copy-start | bytes 12292
  475.8 26.1 %copy-start.127 = (f32[1024]{0:T(1024)}, f32[1024]{0:T(1024)S(1)}, u32[]{:S(2)}) copy-start(f32[1024]{0:T(1024)S(1)} %get-tuple-element.1855) | copy-start | bytes 12292
  475.8 26.1 %copy-start.118 = (f32[1024]{0:T(1024)}, f32[1024]{0:T(1024)S(1)}, u32[]{:S(2)}) copy-start(f32[1024]{0:T(1024)S(1)} %fusion.249) | copy-start | bytes 12292
  517.8 13.5 copy-start.2
  536.8 76.8 %copy-start.40 = (f32[2,32,256]{2,1,0:T(8,128)}, f32[2,32,256]{2,1,0:T(8,128)S(1)}, u32[]{:S(2)}) copy-start(f32[2,32,256]{2,1,0:T(8,128)S(1)} %get-tuple-element.2367) | copy-start | bytes 196612 | tf_op jit(solution)/shard_map/transpose(jvp())/while
  557.1 56.5 %copy-start.44 = (pred[256,256]{1,0:T(8,128)(4,1)}, pred[256,256]{1,0:T(8,128)(4,1)S(1)}, u32[]{:S(2)}) copy-start(pred[256,256]{1,0:T(8,128)(4,1)S(1)} %iota_compare_fusion.5) | copy-start | bytes 196612 | tf_op jit(solution)/shard_map/transpose(jvp())/while
  580.2 9.7 slice-start
  680.7 9.5 slice-start.7
  680.7 9.5 slice-start.8
  680.7 9.5 slice-start.10
  734.6 13.5 copy-start.2
  753.6 76.8 %copy-start.40 = (f32[2,32,256]{2,1,0:T(8,128)}, f32[2,32,256]{2,1,0:T(8,128)S(1)}, u32[]{:S(2)}) copy-start(f32[2,32,256]{2,1,0:T(8,128)S(1)} %get-tuple-element.2367) | copy-start | bytes 196612 | tf_op jit(solution)/shard_map/transpose(jvp())/while
  773.9 56.5 %copy-start.44 = (pred[256,256]{1,0:T(8,128)(4,1)}, pred[256,256]{1,0:T(8,128)(4,1)S(1)}, u32[]{:S(2)}) copy-start(pred[256,256]{1,0:T(8,128)(4,1)S(1)} %iota_compare_fusion.5) | copy-start | bytes 196612 | tf_op jit(solution)/shard_map/transpose(jvp())/while
  797.0 9.7 slice-start
  897.4 9.5 slice-start.7
  897.4 9.5 slice-start.8
  897.4 9.5 slice-start.10
  952.1 11.8 copy-start.119
  952.1 11.8 copy-start.124
  963.9 16.9 copy-start.128
  963.9 16.9 copy-start.33
  963.9 16.9 copy-start.34
  991.0 733.3 %reduce-scatter.11.cloned.1.call-start = ((), (), s32[]{:S(2)}) async-start(), calls=%async_computation.7 | async-start | bytes 5242880 | tf_op jit(solution)/shard_map/reduce_scatter | solution.py:160
  993.6 211.0 %copy-start.137 = (f32[2,512]{1,0:T(2,128)S(1)}, f32[2,512]{1,0:T(2,128)}, u32[]{:S(2)}) copy-start(f32[2,512]{1,0:T(2,128)} %copy-done.136) | copy-start | bytes 12292
  1214.7 509.6 %reduce-scatter.7.cloned.1.call-start = ((), (), s32[]{:S(2)}) async-start(), calls=%async_computation.5 | async-start | bytes 11223040 | tf_op jit(solution)/shard_map/reduce_scatter | solution.py:157
  1231.9 647.5 %reduce-scatter.5.cloned.1.call-start = ((), (), s32[]{:S(2)}) async-start(), calls=%async_computation.4 | async-start | bytes 11223040 | tf_op jit(solution)/shard_map/reduce_scatter | solution.py:157
  1282.1 77.1 %copy-start.42 = (f32[2,32,256]{2,1,0:T(8,128)}, f32[2,32,256]{2,1,0:T(8,128)S(1)}, u32[]{:S(2)}) copy-start(f32[2,32,256]{2,1,0:T(8,128)S(1)} %get-tuple-element.2434) | copy-start | bytes 196612 | tf_op jit(solution)/shard_map/transpose(jvp())/while
  1302.3 56.8 %copy-start.46 = (pred[256,256]{1,0:T(8,128)(4,1)}, pred[256,256]{1,0:T(8,128)(4,1)S(1)}, u32[]{:S(2)}) copy-start(pred[256,256]{1,0:T(8,128)(4,1)S(1)} %iota_compare_fusion.6) | copy-start | bytes 196612 | tf_op jit(solution)/shard_map/transpose(jvp())/while
  1325.4 9.8 slice-start.2
  1426.3 9.5 slice-start.12
  1508.7 76.8 %copy-start.42 = (f32[2,32,256]{2,1,0:T(8,128)}, f32[2,32,256]{2,1,0:T(8,128)S(1)}, u32[]{:S(2)}) copy-start(f32[2,32,256]{2,1,0:T(8,128)S(1)} %get-tuple-element.2434) | copy-start | bytes 196612 | tf_op jit(solution)/shard_map/transpose(jvp())/while
  1528.9 56.6 %copy-start.46 = (pred[256,256]{1,0:T(8,128)(4,1)}, pred[256,256]{1,0:T(8,128)(4,1)S(1)}, u32[]{:S(2)}) copy-start(pred[256,256]{1,0:T(8,128)(4,1)S(1)} %iota_compare_fusion.6) | copy-start | bytes 196612 | tf_op jit(solution)/shard_map/transpose(jvp())/while
  1552.1 9.7 slice-start.2
  1724.2 155.3 %copy-start.126 = (f32[1,4,2,128]{3,2,1,0:T(2,128)S(1)}, f32[1,4,2,128]{3,2,1,0:T(2,128)}, u32[]{:S(2)}) copy-start(f32[1,4,2,128]{3,2,1,0:T(2,128)} %get-tuple-element.1839) | copy-start | bytes 12292
  1724.2 269.0 %all-reduce.51.cloned.1.call-start = ((), (), s32[]{:S(2)}) async-start(), calls=%async_computation.13 | async-start | bytes 13172736 | tf_op jit(solution)/shard_map/psum | solution.py:165
  1879.5 240.9 %all-reduce.49.cloned.1.call-start = ((), (), s32[]{:S(2)}) async-start(), calls=%async_computation.8 | async-start | bytes 147456 | tf_op jit(solution)/shard_map/psum | solution.py:181
  1879.6 11.9 copy-start.63
  1879.6 11.9 copy-start.60
  1879.6 11.9 copy-start.122
  1891.5 17.7 copy-start.50
  1891.5 17.7 copy-start.53
  1891.5 18.3 copy-start.98
  1891.5 18.3 copy-start.101
  1891.5 18.4 copy-start.111
  1891.5 18.4 copy-start.117
  1891.6 18.4 copy-start.108
  1891.6 18.4 copy-start.114
  1891.6 18.4 copy-start.71
  1891.6 18.4 copy-start.74
  1891.6 18.4 copy-start.138
  1910.1 49.8 %copy-start.135 = (f32[1,4,2,128]{3,1,2,0:T(4,128)S(1)}, f32[1,4,2,128]{3,1,2,0:T(4,128)}, u32[]{:S(2)}) copy-start(f32[1,4,2,128]{3,1,2,0:T(4,128)} %copy.386) | copy-start | bytes 12292
  (212 other events, 866.9 us)
Sparse Core Ops, SparseCore 0:
  10.5 79.2 all-gather.14
  91.9 156.9 all-gather.8
  250.5 79.2 all-gather.10
  331.2 156.9 all-gather.12
  991.1 77.9 reduce-scatter.8
  1214.8 78.0 reduce-scatter.10
  1295.2 154.1 reduce-scatter.6
  1724.3 155.1 reduce-scatter.4
  1883.2 109.8 all-reduce.50
  1999.2 121.1 all-reduce.48
where the time goes:
time: 2140 us; the launch traced here: 2130 us
  matrix products  667 us (31%)
  waiting for transfers between devices  520 us (24%)
  other arithmetic  425 us (20%)
  local copies, waits for them, and re-layouts  424 us (20%)
  blocking collectives  42.3 us (2%)
  loops' own time  34.9 us (2%)
    dot_general x16, matrix products, span_scan(): intra = jnp.einsum('chqk,ckhp->cqhp', mixing, scaled_x, precision=HIGHEST)  327 us
    all_gather x2, waiting for transfers between devices, per_device(): lax.all_gather(w_in[layer], 'shard', axis=0, tiled=True)  160 us
    reduce_scatter x2, waiting for transfers between devices, per_device(): lax.psum_scatter(local_in.astype(jnp.bfloat16), 'shard', scatter_dimensio...  155 us
    psum x1, waiting for transfers between devices, per_device(): lax.psum((small_local[0], small_local[1], small_local[2], small_local[3],...  118 us
    mul x8, other arithmetic, mix_one(): act = jax.nn.silu(pre_act)  83.6 us
    while x416, local copies, waits for them, and re-layouts  80.3 us
    mul x20, other arithmetic, mix_one(): conv_weight[offset][None, :] * padded[offset:offset + seq_len]  67.5 us
    dot_general x12, matrix products, span_scan(): jnp.einsum('cqn,chpn->cqhp', c_blocks, previous, precision=HIGHEST)  64.9 us
  transfers between devices with their start and end apart: 10, of which 6 were waited for; matrix products, arithmetic and copies ran while one was open for 46% of the time, Pallas kernels for 0%

commit v1 on v0

--- a/solution.py
+++ b/solution.py
@@ -179,16 +179,19 @@
         jnp.stack([item[5] for item in extra_parts]),
     )
     summed = lax.psum(
-        (
-            small_local[0],
-            small_local[1],
-            small_local[2],
-            small_local[3],
-            small_local[4],
-            small_local[5],
-            small_local[6],
+        lax.psum(
+            (
+                small_local[0],
+                small_local[1],
+                small_local[2],
+                small_local[3],
+                small_local[4],
+                small_local[5],
+                small_local[6],
+            ),
+            "shard",
         ),
-        ("replica", "shard"),
+        "replica",
     )
     return (
         hidden.reshape(slot_count, seq_len, width),

time: 2140 us -> 2110 us (0.986)
  waiting for transfers between devices: 520 us -> 488 us
    psum x1, waiting for transfers between devices: 118 us -> 0.01 us  [per_device(): lax.psum((small_local[0], small_local[1], small_local[2], small_local[3],...]
    psum x1, waiting for transfers between devices: 21.3 us -> 76.8 us  [per_device(): lax.psum(owned_in.astype(jnp.bfloat16), 'replica').astype(jnp.float32)]
    psum x0 -> x1, waiting for transfers between devices: none -> 44.1 us  [per_device(): lax.psum(lax.psum((small_local[0], small_local[1], small_local[2], small_...]
    psum x1, blocking collectives: 42.3 us -> 15.9 us  [per_device(): lax.psum((small_local[0], small_local[1], small_local[2], small_local[3],...]
    psum x0 -> x1, blocking collectives: none -> 24 us  [per_device(): lax.psum(lax.psum((small_local[0], small_local[1], small_local[2], small_...]
  transfers between devices with their start and end apart: 10 -> 11, of which waited for: 6 -> 6; matrix products, arithmetic and copies ran while one was open for 46% -> 46% of each run, Pallas kernels for 0% -> 0%
where the time goes in v1:
time: 2110 us; the launch traced here: 2090 us
  matrix products  661 us (31%)
  waiting for transfers between devices  488 us (23%)
  local copies, waits for them, and re-layouts  427 us (20%)
  other arithmetic  425 us (20%)
  blocking collectives  39.9 us (2%)
  loops' own time  34.8 us (2%)
    dot_general x16, matrix products, span_scan(): intra = jnp.einsum('chqk,ckhp->cqhp', mixing, scaled_x, precision=HIGHEST)  327 us
    all_gather x2, waiting for transfers between devices, per_device(): lax.all_gather(w_in[layer], 'shard', axis=0, tiled=True)  160 us
    reduce_scatter x2, waiting for transfers between devices, per_device(): lax.psum_scatter(local_in.astype(jnp.bfloat16), 'shard', scatter_dimensio...  142 us
    mul x8, other arithmetic, mix_one(): act = jax.nn.silu(pre_act)  83.6 us
    while x416, local copies, waits for them, and re-layouts  80.3 us
    psum x1, waiting for transfers between devices, per_device(): lax.psum(owned_in.astype(jnp.bfloat16), 'replica').astype(jnp.float32)  76.8 us
    mul x20, other arithmetic, mix_one(): conv_weight[offset][None, :] * padded[offset:offset + seq_len]  67.5 us
    dot_general x12, matrix products, span_scan(): jnp.einsum('cqn,chpn->cqhp', c_blocks, previous, precision=HIGHEST)  64.9 us
  transfers between devices with their start and end apart: 11, of which 6 were waited for; matrix products, arithmetic and copies ran while one was open for 46% of the time, Pallas kernels for 0%

profile of v1, /device:TPU:8, one launch (start us, length us, event | category | flops | bytes accessed | tf_op | source)
XLA Modules:
  0.0 2091.7 jit_solution(11248590826619335543)
XLA Ops:
  25.7 64.1 %all-gather.15.cloned.1.call-done = bf16[1,2048,1024]{2,1,0:T(8,128)(2,1)} async-done(((bf16[1,512,1024]{2,1,0:T(8,128)(2,1)}), bf16[1,2048,1024]{2,1,0:T(8,128)(2,1)}) %all-gather.15.cloned.1.call-update) | async-done | bytes 4194320 | tf_op jit(solution)/shard_map/all_gather | solution.py:118
  89.8 11.7 fusion.234
  101.5 147.4 %all-gather.9.cloned.1.call-done = bf16[1,1024,4384]{1,2,0:T(8,128)(2,1)} async-done(((bf16[1,256,4384]{1,2,0:T(8,128)(2,1)}), bf16[1,1024,4384]{1,2,0:T(8,128)(2,1)}) %all-gather.9.cloned.1.call-update) | async-done | bytes 8978448 | tf_op jit(solution)/shard_map/all_gather | solution.py:117
  248.9 17.7 fusion.228
  269.1 195.3 %while.84 = (s32[]{:T(128)}, bf16[2,512,2048]{2,1,0:T(8,128)(2,1)}, f32[1,2304]{1,0:T(1,128)S(1)}, f32[1,2304]{1,0:T(1,128)S(1)}, f32[2,512,4384]{1,2,0:T(8,128)...) while((s32[]{:T(128)}, bf16[2,512,2048]{2,1,0:T(8,128)(2,1)}, ...), condition=%wide.region_5.6_spmd.clone.clone, body=%wide.region_1.5_spmd.clone.clone.sunk | while | flops 5888705024 | bytes 198113264 | solution.py:79
  284.8 12.7 divide_multiply_fusion.4
  308.1 11.1 broadcast_multiply_fusion.29
  325.1 20.4 fusion.414
  382.2 12.7 divide_multiply_fusion.4
  405.5 11.1 broadcast_multiply_fusion.29
  422.6 20.4 fusion.414
  464.5 11.2 multiply_reduce_fusion.34
  475.8 12.4 all-gather.13.cloned.1.call-done
  488.2 13.7 fusion.226
  512.7 439.3 %while.86 = (s32[]{:T(128)}, f32[2304]{0:T(1024)}, f32[4,2304]{1,0:T(4,128)}, f32[32]{0:T(128)}, f32[32]{0:T(128)}, /*index=5*/f32[32]{0:T(128)}, f32[2048]{0:T(...) while((s32[]{:T(128)}, f32[2304]{0:T(1024)}, ...), condition=%wide.region_37.39_spmd.clone, body=%wide.region_12.38_spmd.clone.sunk | while | flops 18517338112 | bytes 734076864 | solution.py:79
  523.1 8.2 fusion.448
  557.1 19.7 bitcast_add_fusion.17
  604.7 8.9 fusion.457
  613.6 26.5 %fusion.456 = (f32[2,32,256]{2,1,0:T(8,128)S(1)}, f32[2,32,256]{2,1,0:T(8,128)}, f32[2,256,256]{2,1,0:T(8,128)S(1)}) fusion(f32[2,256,256]{2,1,0:T(8,128)S(1)} %fusion.452, f32[2,32,256]{2,1,0:T(8,128)S(1)} %get-tuple-element.2373, pred[256,256]{1,0:T(8,128)(4,1)S(1)} %iota_compare_fusion.5, f32[2,256,32,64]{1,0,3,2:T(2,128)} %reshape.1287, ...), kind=kOutput, calls=%fused_computation.112.clone.1 | convolution fusion | flops 3268247552 | bytes 9764864 | tf_op jit(solution)/shard_map/transpose(jvp())/while/body/eval_jaxpr/checkpoint/chqk,ckhp->cqhp/dot_general | solution.py:37
  660.0 15.0 bitcast_add_fusion.18
  690.2 10.1 broadcast_multiply_fusion.34
  700.3 7.9 pad_add_fusion.8
  739.9 8.2 fusion.448
  773.9 19.7 bitcast_add_fusion.17
  821.5 8.9 fusion.457
  830.4 26.5 %fusion.456 = (f32[2,32,256]{2,1,0:T(8,128)S(1)}, f32[2,32,256]{2,1,0:T(8,128)}, f32[2,256,256]{2,1,0:T(8,128)S(1)}) fusion(f32[2,256,256]{2,1,0:T(8,128)S(1)} %fusion.452, f32[2,32,256]{2,1,0:T(8,128)S(1)} %get-tuple-element.2373, pred[256,256]{1,0:T(8,128)(4,1)S(1)} %iota_compare_fusion.5, f32[2,256,32,64]{1,0,3,2:T(2,128)} %reshape.1287, ...), kind=kOutput, calls=%fused_computation.112.clone.1 | convolution fusion | flops 3268247552 | bytes 9764864 | tf_op jit(solution)/shard_map/transpose(jvp())/while/body/eval_jaxpr/checkpoint/chqk,ckhp->cqhp/dot_general | solution.py:37
  876.8 15.0 bitcast_add_fusion.18
  907.0 10.1 broadcast_multiply_fusion.34
  917.1 7.9 pad_add_fusion.8
  952.1 11.8 copy.326
  963.9 16.9 multiply_reduce_fusion.32
  993.6 211.0 %while.85 = (s32[]{:T(128)}, bf16[2,512,2048]{2,1,0:T(8,128)(2,1)}, f32[1,2304]{1,0:T(1,128)S(1)}, f32[1,2304]{1,0:T(1,128)S(1)}, f32[2,512,4384]{1,2,0:T(8,128)...) while((s32[]{:T(128)}, bf16[2,512,2048]{2,1,0:T(8,128)(2,1)}, ...), condition=%wide.region_11.12_spmd.clone.clone, body=%wide.region_7.11_spmd.clone.clone.sunk | while | flops 5888705024 | bytes 198113264 | solution.py:79
  1025.2 12.7 divide_multiply_fusion.5
  1048.4 11.1 broadcast_multiply_fusion.31
  1065.4 20.4 fusion.427
  1122.4 12.7 divide_multiply_fusion.5
  1145.6 11.0 broadcast_multiply_fusion.31
  1162.5 20.4 fusion.427
  1204.6 10.1 bitcast_convert_fusion.1
  1215.4 16.5 convolution_convert_fusion
  1232.6 11.4 fusion.238
  1248.2 460.1 %while.87 = (s32[]{:T(128)}, f32[2304]{0:T(1024)}, f32[4,2304]{1,0:T(4,128)}, f32[32]{0:T(128)}, f32[32]{0:T(128)}, /*index=5*/f32[32]{0:T(128)}, f32[2048]{0:T(...) while((s32[]{:T(128)}, f32[2304]{0:T(1024)}, ...), condition=%wide.region_64.66_spmd.clone, body=%wide.region_39.65_spmd.clone.sunk | while | flops 18517338112 | bytes 706551744 | solution.py:79
  1248.4 8.3 dynamic-slice_bitcast_fusion.14
  1268.4 8.2 fusion.480
  1302.3 19.7 bitcast_add_fusion.19
  1350.2 8.9 fusion.489
  1359.2 26.5 %fusion.488 = (f32[2,32,256]{2,1,0:T(8,128)S(1)}, f32[2,32,256]{2,1,0:T(8,128)}, f32[2,256,256]{2,1,0:T(8,128)S(1)}) fusion(f32[2,256,256]{2,1,0:T(8,128)S(1)} %fusion.484, f32[2,32,256]{2,1,0:T(8,128)S(1)} %get-tuple-element.2440, pred[256,256]{1,0:T(8,128)(4,1)S(1)} %iota_compare_fusion.6, f32[2,256,32,64]{1,0,3,2:T(2,128)} %reshape.1293, ...), kind=kOutput, calls=%fused_computation.257.clone.1 | convolution fusion | flops 3268247552 | bytes 9764864 | tf_op jit(solution)/shard_map/transpose(jvp())/while/body/eval_jaxpr/checkpoint/chqk,ckhp->cqhp/dot_general | solution.py:37
  1405.7 15.0 bitcast_add_fusion.20
  1435.9 10.0 broadcast_multiply_fusion.37
  1475.2 8.3 dynamic-slice_bitcast_fusion.14
  1495.0 8.2 fusion.480
  1528.9 19.7 bitcast_add_fusion.19
  1576.7 8.9 fusion.489
  1585.6 26.5 %fusion.488 = (f32[2,32,256]{2,1,0:T(8,128)S(1)}, f32[2,32,256]{2,1,0:T(8,128)}, f32[2,256,256]{2,1,0:T(8,128)S(1)}) fusion(f32[2,256,256]{2,1,0:T(8,128)S(1)} %fusion.484, f32[2,32,256]{2,1,0:T(8,128)S(1)} %get-tuple-element.2440, pred[256,256]{1,0:T(8,128)(4,1)S(1)} %iota_compare_fusion.6, f32[2,256,32,64]{1,0,3,2:T(2,128)} %reshape.1293, ...), kind=kOutput, calls=%fused_computation.257.clone.1 | convolution fusion | flops 3268247552 | bytes 9764864 | tf_op jit(solution)/shard_map/transpose(jvp())/while/body/eval_jaxpr/checkpoint/chqk,ckhp->cqhp/dot_general | solution.py:37
  1632.0 15.0 bitcast_add_fusion.20
  1662.2 10.0 broadcast_multiply_fusion.37
  1708.3 15.7 bitcast_convert_fusion
  1725.5 12.1 copy.328
  1737.6 141.7 %reduce-scatter.5.cloned.1.call-done = bf16[256,4384]{0,1:T(8,128)(2,1)} async-done(((bf16[1024,4384]{0,1:T(8,128)(2,1)}), bf16[256,4384]{0,1:T(8,128)(2,1)}) %reduce-scatter.5.cloned.1.call-update) | async-done | bytes 2244624 | tf_op jit(solution)/shard_map/reduce_scatter | solution.py:157
  1879.5 17.4 fusion.244
  1897.1 15.9 all-reduce.45
  1913.0 24.0 %all-reduce.44 = (f32[2,1024]{1,0:T(2,128)}, f32[2,2304]{1,0:T(2,128)}, f32[2,2048]{1,0:T(2,128)}, f32[2,32]{1,0:T(2,128)}, f32[2,32]{1,0:T(2,128)}, /*index=5*/f32[2,32]{1,0:T(2,128)}) all-reduce(f32[2,1024]{1,0:T(2,128)S(1)} %get-tuple-element.1723, ...), channel_id=1, replica_groups=mesh['replica'=8,'shard'=4] {'replica'}, use_global_device_ids=true, to_apply=%region_77.79 | all-reduce | flops 10944 | bytes 87552 | tf_op jit(solution)/shard_map/psum | solution.py:181
  1953.3 76.8 %all-reduce.55.cloned.1.call-done = (bf16[1,256,4384]{1,2,0:T(8,128)(2,1)}, bf16[1,256,4384]{1,2,0:T(8,128)(2,1)}, bf16[1,512,1024]{2,1,0:T(8,128)(2,1)}, bf16[1,512,1024]{2,1,0:T(8,128)(2,1)}) async-done(((bf16[1,256,4384]{1,2,0:T(8,128)(2,1)}, bf16[1,256,4384]{1,2,0:T(8,128)(2,1)}, bf16[1,512,1024]{2,1,0:T(8,128)(2,1)}, bf16[1,512,1024]{2,1,0:T(8,128)(2,1)}), (bf16[1,256,4384]{1,2,0:T(8,128)(2,1)}, ...) | async-done | bytes 6586384 | tf_op jit(solution)/shard_map/psum | solution.py:165
  2039.0 44.1 %all-reduce.53.cloned.1.call-done = f32[2,4,2304]{2,1,0:T(4,128)} async-done(((f32[2,4,2304]{2,1,0:T(4,128)}), f32[2,4,2304]{2,1,0:T(4,128)}) %all-reduce.53.cloned.1.call-update) | async-done | bytes 73744 | tf_op jit(solution)/shard_map/psum | solution.py:181
  (1083 shorter events, 786.4 us)
Async XLA Ops:
  7.2 82.6 %all-gather.15.cloned.1.call-start = ((), (), s32[]{:S(2)}) async-start(), calls=%async_computation.13 | async-start | bytes 5242880 | tf_op jit(solution)/shard_map/all_gather | solution.py:118
  10.3 238.6 %all-gather.9.cloned.1.call-start = ((), (), s32[]{:S(2)}) async-start(), calls=%async_computation.10 | async-start | bytes 11223040 | tf_op jit(solution)/shard_map/all_gather | solution.py:117
  15.2 9.9 copy-start.142
  15.2 9.9 copy-start.143
  15.2 449.3 %all-gather.11.cloned.1.call-start = ((), (), s32[]{:S(2)}) async-start(), calls=%async_computation.11 | async-start | bytes 5242880 | tf_op jit(solution)/shard_map/all_gather | solution.py:118
  15.9 472.3 %all-gather.13.cloned.1.call-start = ((), (), s32[]{:S(2)}) async-start(), calls=%async_computation.12 | async-start | bytes 11223040 | tf_op jit(solution)/shard_map/all_gather | solution.py:117
  16.5 1721.1 %reduce-scatter.9.cloned.1.call-start = ((), (), s32[]{:S(2)}) async-start(), calls=%async_computation.6 | async-start | bytes 5242880 | tf_op jit(solution)/shard_map/reduce_scatter | solution.py:160
  18.5 230.4 %copy-start.123 = (f32[1,1024]{1,0:T(1,128)}, f32[1,1024]{1,0:T(1,128)S(1)}, u32[]{:S(2)}) copy-start(f32[1,1024]{1,0:T(1,128)S(1)} %get-tuple-element.1844) | copy-start | bytes 12292
  22.1 226.9 %copy-start.133 = (f32[2,512]{1,0:T(2,128)}, f32[2,512]{1,0:T(2,128)S(1)}, u32[]{:S(2)}) copy-start(f32[2,512]{1,0:T(2,128)S(1)} %get-tuple-element.1846) | copy-start | bytes 12292
  24.5 76.9 %copy-start.138 = (f32[2,512]{1,0:T(2,128)}, f32[2,512]{1,0:T(2,128)S(1)}, u32[]{:S(2)}) copy-start(f32[2,512]{1,0:T(2,128)S(1)} %get-tuple-element.1859) | copy-start | bytes 12292
  269.1 195.4 %copy-start.134 = (f32[1,4,2,128]{3,1,2,0:T(4,128)S(1)}, f32[1,4,2,128]{3,1,2,0:T(4,128)}, u32[]{:S(2)}) copy-start(f32[1,4,2,128]{3,1,2,0:T(4,128)} %copy.386) | copy-start | bytes 12292
  464.5 11.3 copy-start.37
  464.5 11.3 copy-start.78
  464.5 23.7 %copy-start.125 = (f32[1,1024]{1,0:T(1,128)S(1)}, f32[1,1024]{1,0:T(1,128)}, u32[]{:S(2)}) copy-start(f32[1,1024]{1,0:T(1,128)} %get-tuple-element.1843) | copy-start | bytes 12292
  475.8 26.1 %copy-start.129 = (f32[1024]{0:T(1024)}, f32[1024]{0:T(1024)S(1)}, u32[]{:S(2)}) copy-start(f32[1024]{0:T(1024)S(1)} %get-tuple-element.1861) | copy-start | bytes 12292
  475.8 26.1 %copy-start.120 = (f32[1024]{0:T(1024)}, f32[1024]{0:T(1024)S(1)}, u32[]{:S(2)}) copy-start(f32[1024]{0:T(1024)S(1)} %fusion.249) | copy-start | bytes 12292
  517.8 13.5 copy-start.2
  536.8 76.8 %copy-start.42 = (f32[2,32,256]{2,1,0:T(8,128)}, f32[2,32,256]{2,1,0:T(8,128)S(1)}, u32[]{:S(2)}) copy-start(f32[2,32,256]{2,1,0:T(8,128)S(1)} %get-tuple-element.2373) | copy-start | bytes 196612 | tf_op jit(solution)/shard_map/transpose(jvp())/while
  557.1 56.5 %copy-start.46 = (pred[256,256]{1,0:T(8,128)(4,1)}, pred[256,256]{1,0:T(8,128)(4,1)S(1)}, u32[]{:S(2)}) copy-start(pred[256,256]{1,0:T(8,128)(4,1)S(1)} %iota_compare_fusion.5) | copy-start | bytes 196612 | tf_op jit(solution)/shard_map/transpose(jvp())/while
  580.2 9.7 slice-start
  680.7 9.5 slice-start.7
  680.7 9.5 slice-start.8
  680.7 9.5 slice-start.10
  734.6 13.5 copy-start.2
  753.6 76.8 %copy-start.42 = (f32[2,32,256]{2,1,0:T(8,128)}, f32[2,32,256]{2,1,0:T(8,128)S(1)}, u32[]{:S(2)}) copy-start(f32[2,32,256]{2,1,0:T(8,128)S(1)} %get-tuple-element.2373) | copy-start | bytes 196612 | tf_op jit(solution)/shard_map/transpose(jvp())/while
  773.9 56.5 %copy-start.46 = (pred[256,256]{1,0:T(8,128)(4,1)}, pred[256,256]{1,0:T(8,128)(4,1)S(1)}, u32[]{:S(2)}) copy-start(pred[256,256]{1,0:T(8,128)(4,1)S(1)} %iota_compare_fusion.5) | copy-start | bytes 196612 | tf_op jit(solution)/shard_map/transpose(jvp())/while
  797.0 9.7 slice-start
  897.4 9.5 slice-start.7
  897.4 9.5 slice-start.8
  897.4 9.5 slice-start.10
  952.1 11.8 copy-start.121
  952.1 11.8 copy-start.126
  963.9 16.9 copy-start.130
  963.9 16.9 copy-start.34
  963.9 16.9 copy-start.35
  991.0 746.7 %reduce-scatter.11.cloned.1.call-start = ((), (), s32[]{:S(2)}) async-start(), calls=%async_computation.7 | async-start | bytes 5242880 | tf_op jit(solution)/shard_map/reduce_scatter | solution.py:160
  993.6 211.0 %copy-start.139 = (f32[2,512]{1,0:T(2,128)S(1)}, f32[2,512]{1,0:T(2,128)}, u32[]{:S(2)}) copy-start(f32[2,512]{1,0:T(2,128)} %copy-done.138) | copy-start | bytes 12292
  1214.7 522.9 %reduce-scatter.7.cloned.1.call-start = ((), (), s32[]{:S(2)}) async-start(), calls=%async_computation.5 | async-start | bytes 11223040 | tf_op jit(solution)/shard_map/reduce_scatter | solution.py:157
  1231.9 647.4 %reduce-scatter.5.cloned.1.call-start = ((), (), s32[]{:S(2)}) async-start(), calls=%async_computation.4 | async-start | bytes 11223040 | tf_op jit(solution)/shard_map/reduce_scatter | solution.py:157
  1282.1 77.1 %copy-start.44 = (f32[2,32,256]{2,1,0:T(8,128)}, f32[2,32,256]{2,1,0:T(8,128)S(1)}, u32[]{:S(2)}) copy-start(f32[2,32,256]{2,1,0:T(8,128)S(1)} %get-tuple-element.2440) | copy-start | bytes 196612 | tf_op jit(solution)/shard_map/transpose(jvp())/while
  1302.3 56.8 %copy-start.48 = (pred[256,256]{1,0:T(8,128)(4,1)}, pred[256,256]{1,0:T(8,128)(4,1)S(1)}, u32[]{:S(2)}) copy-start(pred[256,256]{1,0:T(8,128)(4,1)S(1)} %iota_compare_fusion.6) | copy-start | bytes 196612 | tf_op jit(solution)/shard_map/transpose(jvp())/while
  1325.4 9.8 slice-start.2
  1426.3 9.5 slice-start.5
  1426.3 9.5 slice-start.12
  1508.7 76.8 %copy-start.44 = (f32[2,32,256]{2,1,0:T(8,128)}, f32[2,32,256]{2,1,0:T(8,128)S(1)}, u32[]{:S(2)}) copy-start(f32[2,32,256]{2,1,0:T(8,128)S(1)} %get-tuple-element.2440) | copy-start | bytes 196612 | tf_op jit(solution)/shard_map/transpose(jvp())/while
  1528.9 56.6 %copy-start.48 = (pred[256,256]{1,0:T(8,128)(4,1)}, pred[256,256]{1,0:T(8,128)(4,1)S(1)}, u32[]{:S(2)}) copy-start(pred[256,256]{1,0:T(8,128)(4,1)S(1)} %iota_compare_fusion.6) | copy-start | bytes 196612 | tf_op jit(solution)/shard_map/transpose(jvp())/while
  1552.1 9.7 slice-start.2
  1652.7 9.5 slice-start.12
  1724.0 229.3 %all-reduce.51.cloned.1.call-start = ((), (), s32[]{:S(2)}) async-start(), calls=%async_computation.8 | async-start | bytes 147456 | tf_op jit(solution)/shard_map/psum | solution.py:182
  1725.5 304.6 %all-reduce.55.cloned.1.call-start = ((), (), s32[]{:S(2)}) async-start(), calls=%async_computation.14 | async-start | bytes 13172736 | tf_op jit(solution)/shard_map/psum | solution.py:165
  1737.6 141.8 %copy-start.124 = (f32[1,1024]{1,0:T(1,128)S(1)}, f32[1,1024]{1,0:T(1,128)}, u32[]{:S(2)}) copy-start(f32[1,1024]{1,0:T(1,128)} %copy-done.123) | copy-start | bytes 12292
  1879.3 203.8 %all-reduce.53.cloned.1.call-start = ((), (), s32[]{:S(2)}) async-start(), calls=%async_computation.9 | async-start | bytes 147456 | tf_op jit(solution)/shard_map/psum | solution.py:181
  1879.4 17.5 copy-start.65
  1879.4 17.5 copy-start.62
  1879.4 17.5 copy-start.100
  1879.4 17.5 copy-start.103
  1879.4 17.5 copy-start.113
  1879.4 17.5 copy-start.119
  1879.4 17.5 copy-start.110
  1879.5 17.5 copy-start.116
  1879.5 17.5 copy-start.140
  1879.5 17.6 copy-start.73
  1879.5 17.6 copy-start.76
  1937.0 10.3 copy-start.145
  (216 other events, 876.6 us)
Sparse Core Ops, SparseCore 0:
  10.5 79.2 all-gather.14
  91.9 156.9 all-gather.8
  250.5 79.2 all-gather.10
  331.2 156.9 all-gather.12
  991.1 77.9 reduce-scatter.8
  1214.8 78.0 reduce-scatter.10
  1295.2 154.1 reduce-scatter.6
  1724.1 155.1 reduce-scatter.4
  1882.2 35.2 all-reduce.50
  1921.6 108.4 all-reduce.54
  2033.5 49.6 all-reduce.52
